TPU v7x, 32 devices: a whole 2x2x4 slice. The times are simulated.
32 devices in a mesh: elem: 8 (over z, x), inner: 4 (over y, core).
Axes of the slice: x: 2, y: 2, z: 4, core: 2. Of those that a mesh axis runs over, the one named last changes fastest.
Arguments:
- basis: bfloat16 [16, 4, 512, 4096], P('elem', None, 'inner'), may hold values from -6 to 6, as said below
- potential: float32 [16, 4096], P('elem'), may hold values from 0.2 to 2
- face_index: int32 [16, 2, 128], P('elem'), may hold values from 0 to 4095, as said below
- face_match: int32 [16, 128], P('elem'), may hold values from 0 to 127, each once within a row
- vectors: bfloat16 [16, 512, 1024], P('elem', None, 'inner'), may hold values from -6 to 6
Outputs:
- filtered: float32 [16, 512, 1024], P('elem', None, 'inner')
Inputs may be any that keep to these rules, and one draw needn't show every extreme that they name: `basis`: entries are independent, of mean zero and variance one. `face_index`: within one element the 256 listed grid points are distinct. Row e is a permutation; right-face point f of element e - 1 (modulo 16) meets left-face point face_match[e, f] of element e.
All inputs are finite; a program needn't handle non-finite values.
Results may differ from a plain program's by a relative error of at most 0.007.
The roundings to bfloat16 on the way count: a program that leaves them out, or rounds other values in their place, can miss the bound.
Values may be sent and summed in bfloat16 or wider, within the bound.
A program may use at most 64 MiB of HBM per device.

v0:
```python
import functools

import jax
import jax.numpy as jnp
from jax import lax
from jax.experimental import pallas as pl
from jax.experimental.pallas import tpu as pltpu
from jax.sharding import PartitionSpec as P

MESH = pl.DeviceIdType.MESH

NG = 4096
F = 128
STEPS = 6


CENTER = 5.25
HALF_WIDTH = 2.75


def padded_2(cells, sides, width):
    for axis, dim in sides:
        count = lax.axis_size(axis)
        head = lax.slice_in_dim(cells, 0, width, axis=dim)
        tail = lax.slice_in_dim(cells, cells.shape[dim] - width, cells.shape[dim], axis=dim)
        cells = jnp.concatenate(
            [
                lax.ppermute(tail, axis, [(i, (i + 1) % count) for i in range(count)]),
                cells,
                lax.ppermute(head, axis, [((i + 1) % count, i) for i in range(count)]),
            ],
            axis=dim,
        )
    return cells


def chebyshev_norm(count):
    ratio = (CENTER - 1.0) / HALF_WIDTH
    root = ratio + (ratio * ratio - 1.0) ** 0.5
    return 0.5 * (root**count + root ** (-count))


def face_pair(leading, second):
    return jnp.einsum(
        "nsaf,nsbf->nab", leading, jnp.flip(second, 1), preferred_element_type=jnp.float32
    ) / (4.0 * F)


def gram_terms(exchanged):
    scaled = exchanged[:, 0]
    slopes = exchanged[:, 1:4]
    volume = jnp.einsum("nag,nbg->nab", scaled, scaled, preferred_element_type=jnp.float32)
    kinetic = jnp.einsum("ncag,ncbg->nab", slopes, slopes, preferred_element_type=jnp.float32)
    return (volume + 0.5 * kinetic) / NG


def face_values(element_block, element_points):
    return jnp.take(element_block[0:2], element_points, axis=2)


def per_device(basis, potential, face_index, face_match, vectors):
    elements = basis.shape[0]
    scaled = (jnp.sqrt(potential)[:, None, :] * basis[:, 0].astype(jnp.float32)).astype(
        jnp.bfloat16
    )
    grid_pack = jnp.concatenate((scaled[:, None], basis[:, 1:4]), axis=1)
    gram_part = gram_terms(
        lax.all_to_all(grid_pack, "inner", split_axis=3, concat_axis=2, tiled=True)
    )
    left_points = jnp.take_along_axis(face_index[:, 0, :], face_match, axis=1)
    right_found = jax.vmap(face_values)(basis, face_index[:, 1, :])
    left_found = jax.vmap(face_values)(basis, left_points)
    right_flux = (
        0.5 * right_found[:, 0].astype(jnp.float32) - 0.25 * right_found[:, 1].astype(jnp.float32)
    ).astype(jnp.bfloat16)
    left_flux = (
        -0.5 * left_found[:, 0].astype(jnp.float32) - 0.25 * left_found[:, 1].astype(jnp.float32)
    ).astype(jnp.bfloat16)
    right_sides = jnp.stack((right_flux, right_found[:, 0]), axis=1)
    left_sides = jnp.stack((left_flux, -left_found[:, 0]), axis=1)
    rim_sides = jnp.stack((left_sides[0], right_sides[-1]))
    rim_padded = padded_2(rim_sides, (("elem", 0),), 1)
    from_left = rim_padded[0:1]
    from_right = rim_padded[3:4]
    local_sides = jnp.concatenate((right_sides, left_sides, from_left, from_right), axis=0)
    full_sides = lax.all_gather(local_sides, "inner", axis=2, tiled=True)
    full_rights = full_sides[:elements]
    full_lefts = full_sides[elements : 2 * elements]
    full_next = full_sides[2 * elements + 1 : 2 * elements + 2]
    full_prev = full_sides[2 * elements : 2 * elements + 1]
    next_lefts = jnp.concatenate((full_lefts[1:], full_next), axis=0)
    gram_sum = lax.psum(gram_part, "inner")
    diagonal = (
        gram_sum + face_pair(full_rights, full_rights) + face_pair(full_lefts, full_lefts)
    ).astype(jnp.bfloat16)
    upper_blocks = face_pair(full_rights, next_lefts).astype(jnp.bfloat16)
    first_lower = face_pair(full_prev, full_lefts[0:1]).astype(jnp.bfloat16)
    lower_blocks = jnp.concatenate((first_lower, upper_blocks[:-1]), axis=0)

    def apply_operator(current_bf):
        padded = padded_2(current_bf, (("elem", 0),), 1)
        result = jnp.einsum(
            "jab,jbv->jav", diagonal, current_bf, preferred_element_type=jnp.float32
        )
        result = result + jnp.einsum(
            "jab,jbv->jav", upper_blocks, padded[2:], preferred_element_type=jnp.float32
        )
        result = result + jnp.einsum(
            "jba,jbv->jav", lower_blocks, padded[:-2], preferred_element_type=jnp.float32
        )
        return result

    previous = vectors.astype(jnp.float32)
    current = (apply_operator(vectors) - CENTER * previous) / HALF_WIDTH
    for iteration in range(1, STEPS):
        applied = apply_operator(current.astype(jnp.bfloat16))
        following = 2.0 * (applied - CENTER * current) / HALF_WIDTH - previous
        previous = current
        current = following
    return current / chebyshev_norm(STEPS)


def assemble_and_filter(
    inner,
    ring,
    basis,
    potential,
    face_index,
    face_match,
    vectors,
    out,
    own,
    cross,
    nodal,
    faces,
    after,
    before,
    operator,
    own_sum,
    cross_sum,
    own_other,
    cross_other,
    state,
    current,
    previous,
    local_sem,
    pair_send,
    pair_recv,
    cross_send,
    cross_recv,
    face_send,
    face_recv,
    rim_send,
    rim_recv,
    sum_send,
    sum_recv,
    block_send,
    block_recv,
    halo_send,
    halo_recv,
):
    elements, parts, rows, grid = basis.shape
    total = rows * inner
    faced = face_index.shape[2]
    half = grid // 2
    step_k = min(half, 512)
    columns = vectors.shape[2] // 2
    me = lax.axis_index("inner")
    place = lax.axis_index("elem")
    chip, core = me // 2, lax.rem(me, 2)
    partner = chip * 2 + (1 - core)
    far = 1 - chip
    following = lax.rem(place + 1, ring)
    preceding = lax.rem(place + ring - 1, ring)
    peers = [lax.rem(me + d, inner) for d in range(1, inner)]
    across = far * 2 + core
    diagonal_peer = far * 2 + (1 - core)
    routes = ((0, partner), (1, across))
    sources = (partner, across, diagonal_peer)

    def aligned(index, size):
        return pl.ds(pl.multiple_of(index * size, size), size)

    def send(src, dst, send_sem, recv_sem, **where):
        return pltpu.make_async_remote_copy(
            src_ref=src,
            dst_ref=dst,
            send_sem=send_sem,
            recv_sem=recv_sem,
            device_id=where,
            device_id_type=MESH,
        )

    barrier = pltpu.get_barrier_semaphore()
    for peer in peers:
        pl.semaphore_signal(barrier, inc=1, device_id={"inner": peer}, device_id_type=MESH)
    for peer in (preceding, following):
        pl.semaphore_signal(barrier, inc=1, device_id={"elem": peer}, device_id_type=MESH)

    nodal_copy = pltpu.make_async_copy(basis.at[:, 0:2], nodal, local_sem.at[0, 0])
    nodal_copy.start()
    local = {}
    for e in range(elements):
        for k in range(parts):
            local[e, k] = pltpu.make_async_copy(
                basis.at[e, k, :, aligned(core, half)],
                own.at[e, k, aligned(core, rows)],
                local_sem.at[1 + e, k],
            )
            local[e, k].start()

    pl.semaphore_wait(barrier, inner + 1)

    sends = []

    def launch(copy):
        copy.start()
        sends.append(copy)

    def start_cross(k):
        for other in range(2):
            side = lax.rem(core + other, 2)
            launch(
                send(
                    basis.at[far, k, :, aligned(side, half)],
                    cross.at[k, aligned(core, rows)],
                    cross_send.at[other, k],
                    cross_recv.at[other, k],
                    inner=far * 2 + side,
                )
            )

    start_cross(0)
    for e in range(elements):
        for k in range(parts):
            launch(
                send(
                    basis.at[e, k, :, aligned(1 - core, half)],
                    own.at[e, k, aligned(core, rows)],
                    pair_send.at[e, k],
                    pair_recv.at[e, k],
                    inner=partner,
                )
            )

    def halo_copies(k, h, to_next, to_previous):
        return (
            send(
                to_next,
                state.at[k, h, pl.ds(0, total)],
                halo_send.at[k, h, 0],
                halo_recv.at[k, h, 0],
                elem=following,
            ),
            send(
                to_previous,
                state.at[k, h, pl.ds((elements + 1) * total, total)],
                halo_send.at[k, h, 1],
                halo_recv.at[k, h, 1],
                elem=preceding,
            ),
        )

    for h in range(2):
        piece = pl.ds(h * columns, columns)
        for copy in halo_copies(0, h, vectors.at[elements - 1, :, piece], vectors.at[0, :, piece]):
            copy.start()

    nodal_copy.wait()
    square = (faced, faced)
    for e in range(elements):
        down = lax.broadcasted_iota(jnp.int32, square, 0)
        along = lax.broadcasted_iota(jnp.int32, square, 1)
        left_row = jnp.broadcast_to(face_index[e, 0:1, :], square)
        left_column = jnp.sum(jnp.where(down == along, left_row, 0), axis=1, keepdims=True)
        matched = jnp.broadcast_to(face_match[e : e + 1, :], square) == down
        left_points = jnp.sum(
            jnp.where(matched, jnp.broadcast_to(left_column, square), 0), axis=0, keepdims=True
        )
        points = jnp.concatenate([face_index[e, 1:2, :], left_points], axis=1)

        def pick(index, found, e=e, points=points):
            offset = pl.multiple_of(index * step_k, step_k)
            spots = lax.broadcasted_iota(jnp.int32, (step_k, 2 * faced), 0) + offset
            chosen = (spots == jnp.broadcast_to(points, spots.shape)).astype(jnp.float32)
            chosen = chosen.astype(jnp.bfloat16)
            return tuple(
                found[k]
                + jnp.dot(
                    nodal[e, k, :, pl.ds(offset, step_k)],
                    chosen,
                    preferred_element_type=jnp.float32,
                )
                for k in range(2)
            )

        start = jnp.zeros((rows, 2 * faced), jnp.float32)
        value, slope = lax.fori_loop(0, grid // step_k, pick, (start, start))
        right_value, left_value = value[:, :faced], value[:, faced:]
        right_slope, left_slope = slope[:, :faced], slope[:, faced:]
        mine = aligned(me, rows)
        pieces = (
            0.5 * right_value - 0.25 * right_slope,
            right_value,
            -0.5 * left_value - 0.25 * left_slope,
            -left_value,
        )
        for index, piece in enumerate(pieces):
            faces[e, mine, index * faced : (index + 1) * faced] = piece.astype(jnp.bfloat16)
    def face_copy(d, e, owner, target):
        block = faces.at[e, aligned(owner, rows)]
        return send(block, block, face_send.at[d, e], face_recv.at[d, e], inner=target)

    for d, peer in routes:
        for e in range(elements):
            launch(face_copy(d, e, me, peer))
    for k in range(1, parts - 1):
        start_cross(k)

    def product(left, right):
        return lax.dot_general(
            left, right, (((1,), (1,)), ((), ())), preferred_element_type=jnp.float32
        )

    def swapped(side):
        cut = [side[:, k * faced : (k + 1) * faced] for k in range(side.shape[1] // faced)]
        order = [k + 1 - 2 * (k % 2) for k in range(len(cut))]
        return jnp.concatenate([cut[k] for k in order], axis=1)

    def weighted(row_left, row_right, left, right, k, target, scale_left):
        @pl.loop(0, half // step_k)
        def _(index):
            offset = pl.multiple_of(index * step_k, step_k)
            span = pl.ds(offset, step_k)
            there = pl.ds(pl.multiple_of(core * half + offset, step_k), step_k)
            one = left[:, span]
            if k == 0 and scale_left:
                root = jnp.sqrt(potential[row_left, there])
                one = (one.astype(jnp.float32) * root).astype(jnp.bfloat16)
                left[:, span] = one
            two = one if right is left else right[:, span]
            if k == 0 and right is not left:
                root = jnp.sqrt(potential[row_right, there])
                two = (two.astype(jnp.float32) * root).astype(jnp.bfloat16)
            term = product(one, two)
            target[...] += term if k == 0 else 0.5 * term

    for e in range(elements):
        own_sum[e] = jnp.zeros(own_sum.shape[1:], jnp.float32)
        for k in range(parts):
            local[e, k].wait()
            send(
                basis.at[e, k, :, aligned(core, half)],
                own.at[e, k, aligned(1 - core, rows)],
                pair_send.at[e, k],
                pair_recv.at[e, k],
                inner=partner,
            ).wait_recv()
            block = own.at[e, k]
            weighted(pl.ds(e, 1), pl.ds(e, 1), block, block, k, own_sum.at[e], True)
        launch(
            send(
                own_sum.at[e, aligned(1 - core, rows)],
                own_other.at[e],
                sum_send.at[e],
                sum_recv.at[e],
                inner=partner,
            )
        )

    for e in range(elements):
        face_copy(1, e, across, across).wait_recv()
        launch(face_copy(2, e, across, partner))
    for e in range(elements):
        face_copy(0, e, partner, partner).wait_recv()
        face_copy(2, e, diagonal_peer, partner).wait_recv()
    right_cut, left_cut = pl.ds(0, 2 * faced), pl.ds(2 * faced, 2 * faced)
    rims = (
        send(
            faces.at[0, :, left_cut], after, rim_send.at[0], rim_recv.at[0], elem=preceding
        ),
        send(
            faces.at[elements - 1, :, right_cut],
            before,
            rim_send.at[1],
            rim_recv.at[1],
            elem=following,
        ),
    )
    for copy in rims:
        launch(copy)

    def diagonal(e, to_chip):
        return product(
            faces[e, aligned(me, rows)], swapped(faces[e, aligned(to_chip, 2 * rows)])
        ) / (4.0 * faced)

    def block_of(e, owner, to_chip):
        offset = pl.multiple_of(total + to_chip * 2 * rows, 2 * rows)
        return operator.at[e, aligned(owner, rows), pl.ds(offset, 2 * rows)]

    def block_copy(d, slot, owner, target):
        owner_chip = owner // 2
        e = slot if slot < elements else owner_chip
        block = block_of(e, owner, owner_chip if slot < elements else 1 - owner_chip)
        return send(
            block, block, block_send.at[d, slot], block_recv.at[d, slot], inner=target
        )

    for e in range(elements):
        send(
            own_sum.at[e, aligned(core, rows)],
            own_other.at[e],
            sum_send.at[e],
            sum_recv.at[e],
            inner=partner,
        ).wait_recv()
        gram = (own_sum[e, aligned(core, rows)] + own_other[e]) / grid
        block_of(e, me, chip)[...] = (gram + diagonal(e, chip)).astype(jnp.bfloat16)
        for d, peer in routes:
            launch(block_copy(d, e, me, peer))
    start_cross(parts - 1)

    for copy in rims:
        copy.wait_recv()

    def between(target, left, right):
        target[...] = (product(left, swapped(right)) / (4.0 * faced)).astype(jnp.bfloat16)

    high = pl.ds(2 * total, total)
    low = pl.ds(0, total)
    for e in range(elements):
        right_side = faces[e, :, right_cut]
        left_side = faces[e, :, left_cut]
        next_left = faces[e + 1, :, left_cut] if e + 1 < elements else after[...]
        last_right = faces[e - 1, :, right_cut] if e else before[...]
        between(operator.at[e, :, high], right_side, next_left)
        between(operator.at[e, :, low], left_side, last_right)

    for h in range(2):
        for e in range(elements):
            piece = vectors[e, :, h * columns : (h + 1) * columns]
            state[0, h, (e + 1) * total : (e + 2) * total] = piece
            current[h, e] = piece.astype(jnp.float32)

    norm = chebyshev_norm(STEPS)
    tile = min(total, 256)
    wide = 2 * rows

    def halo_of(k, h):
        return halo_copies(
            k,
            h,
            state.at[k, h, pl.ds(elements * total, total)],
            state.at[k, h, pl.ds(total, total)],
        )

    def halo_wait(k, h):
        for copy in halo_of(k, h):
            copy.wait()

    def halo_start(k, h):
        for copy in halo_of(k, h):
            copy.start()

    def times(k, h, e, some, begin, length):
        return jnp.dot(
            operator[e, some, begin : begin + length],
            state[k, h, e * total + begin : e * total + begin + length],
            preferred_element_type=jnp.float32,
        )

    def rest(k, h, e, some, begin, length):
        held = out[e, some, h * columns : (h + 1) * columns]
        return held + times(k, h, e, some, begin, length)

    def update(k, h, e, some, applied, first):
        scale = (2.0 if k else 1.0) / HALF_WIDTH
        now = current[h, e, some]
        moved = scale * applied - (scale * CENTER) * now
        if k:
            moved = moved - previous[h, e, some]
        if k + 1 == STEPS:
            out[e, some, h * columns : (h + 1) * columns] = moved * (1.0 / norm)
        else:
            previous[h, e, some] = now
            current[h, e, some] = moved
            target = pl.ds(pl.multiple_of((e + 1) * total + first, tile), tile)
            state[k + 1, h, target] = moved.astype(jnp.bfloat16)

    cross_face = diagonal(chip, far)
    cross_sum[...] = jnp.zeros(cross_sum.shape, jnp.float32)
    for k in range(parts):
        if k + 1 == parts:
            for e in range(elements):
                block_copy(1, e, across, across).wait_recv()
                launch(block_copy(2, e, across, partner))
            for e in range(elements):
                block_copy(0, e, partner, partner).wait_recv()
                block_copy(2, e, diagonal_peer, partner).wait_recv()
            for h in range(2):
                halo_wait(0, h)
                for e in range(elements):
                    for q in range(2):
                        some = slice(q * wide, (q + 1) * wide)
                        held = pl.ds(h * columns, columns)
                        out[e, some, held] = times(0, h, e, some, 0, total + (1 - q) * wide)
                        out[e, some, held] += times(
                            0, h, e, some, 2 * total - q * wide, total + q * wide
                        )
        for other in range(2):
            side = lax.rem(core + other, 2)
            send(
                basis.at[far, k, :, aligned(core, half)],
                cross.at[k, aligned(side, rows)],
                cross_send.at[other, k],
                cross_recv.at[other, k],
                inner=far * 2 + side,
            ).wait_recv()
        weighted(
            pl.ds(chip, 1), pl.ds(chip, 1), own.at[chip, k], cross.at[k], k, cross_sum, False
        )
    final = send(
        cross_sum.at[aligned(1 - core, rows)],
        cross_other,
        sum_send.at[elements],
        sum_recv.at[elements],
        inner=partner,
    )
    launch(final)
    final.wait_recv()
    gram = (cross_sum[aligned(core, rows)] + cross_other[...]) / grid
    block_of(chip, me, far)[...] = (gram + cross_face).astype(jnp.bfloat16)
    for d, peer in enumerate(sources):
        launch(block_copy(d, elements, me, peer))
    for d, source in enumerate(sources):
        block_copy(d, elements, source, source).wait_recv()
    for e in range(elements):
        mine, theirs = e * wide, (1 - e) * wide
        found = operator[e, mine : mine + wide, total + theirs : total + theirs + wide]
        operator[e, theirs : theirs + wide, total + mine : total + mine + wide] = found.T

    for h in range(2):
        for q in range(2):
            some = slice(q * wide, (q + 1) * wide)
            begin = total + (1 - q) * wide
            for e in range(elements):
                update(0, h, e, some, rest(0, h, e, some, begin, wide), q * wide)
        halo_start(1, h)
    for k in range(1, STEPS):
        for h in range(2):

            @pl.loop(0, total // tile)
            def _(index, k=k, h=h):
                some = pl.ds(pl.multiple_of(index * tile, tile), tile)
                for e in range(elements):
                    out[e, some, h * columns : (h + 1) * columns] = times(
                        k, h, e, some, 0 if e else total, 2 * total
                    )

            halo_wait(k, h)

            @pl.loop(0, total // tile)
            def _(index, k=k, h=h):
                first = pl.multiple_of(index * tile, tile)
                some = pl.ds(first, tile)
                for e in range(elements):
                    applied = rest(k, h, e, some, 2 * total if e else 0, total)
                    update(k, h, e, some, applied, first)

            if k + 1 < STEPS:
                halo_start(k + 1, h)

    for copy in sends:
        copy.wait_send()


def fused(inner, ring, basis, potential, face_index, face_match, vectors):
    elements, parts, rows, grid = basis.shape
    total, width = vectors.shape[1], vectors.shape[2]
    faced = face_index.shape[2]
    half = grid // 2
    bf16, f32, dma = jnp.bfloat16, jnp.float32, pltpu.SemaphoreType.DMA
    vmem = pl.BlockSpec(memory_space=pltpu.VMEM)
    return pl.pallas_call(
        functools.partial(assemble_and_filter, inner, ring),
        out_shape=jax.ShapeDtypeStruct(vectors.shape, f32),
        in_specs=[pl.BlockSpec(memory_space=pltpu.HBM)] + [vmem] * 4,
        out_specs=vmem,
        scratch_shapes=[
            pltpu.VMEM((elements, parts, 2 * rows, half), bf16),
            pltpu.VMEM((parts, 2 * rows, half), bf16),
            pltpu.VMEM((elements, 2, rows, grid), bf16),
            pltpu.VMEM((elements, total, 4 * faced), bf16),
            pltpu.VMEM((total, 2 * faced), bf16),
            pltpu.VMEM((total, 2 * faced), bf16),
            pltpu.VMEM((elements, total, 3 * total), bf16),
            pltpu.VMEM((elements, 2 * rows, 2 * rows), f32),
            pltpu.VMEM((2 * rows, 2 * rows), f32),
            pltpu.VMEM((elements, rows, 2 * rows), f32),
            pltpu.VMEM((rows, 2 * rows), f32),
            pltpu.VMEM((STEPS, 2, (elements + 2) * total, width // 2), bf16),
            pltpu.VMEM((2, elements, total, width // 2), f32),
            pltpu.VMEM((2, elements, total, width // 2), f32),
            dma((1 + elements, parts)),
            dma((elements, parts)),
            dma((elements, parts)),
            dma((2, parts)),
            dma((2, parts)),
            dma((inner - 1, elements)),
            dma((inner - 1, elements)),
            dma((2,)),
            dma((2,)),
            dma((elements + 1,)),
            dma((elements + 1,)),
            dma((inner - 1, elements + 1)),
            dma((inner - 1, elements + 1)),
            dma((STEPS, 2, 2)),
            dma((STEPS, 2, 2)),
        ],
        compiler_params=pltpu.CompilerParams(
            collective_id=0, has_side_effects=True, vmem_limit_bytes=60 * 1024 * 1024
        ),
    )(basis, potential, face_index, face_match, vectors)


def solution(mesh):
    inner, ring = mesh.shape["inner"], mesh.shape["elem"]
    placed = (
        P("elem", None, "inner", None),
        P("elem", None),
        P("elem", None, None),
        P("elem", None),
        P("elem", None, "inner"),
    )

    def local(basis, *rest):
        if inner == 4 and basis.shape[0] == 2:
            return fused(inner, ring, basis, *rest)
        return per_device(basis, *rest)

    return jax.shard_map(
        local, mesh=mesh, in_specs=placed, out_specs=P("elem", None, "inner"), check_vma=False
    )
```

profile of v0, /device:TPU:0, one launch (start us, length us, event | category | flops | bytes accessed | tf_op | source)
XLA Modules:
  0.0 176.8 jit_solution(16751442994836854383)
XLA Ops:
  0.0 174.5 %shard_map.55 = f32[2,512,256]{2,1,0:T(8,128)} custom-call(bf16[2,4,128,4096]{3,2,1,0:T(8,128)(2,1)} %basis.1, f32[2,4096]{1,0:T(2,128)} %potential.1, s32[2,2,128]{2,1,0:T(2,128)} %face_index.1, s32[2,128]{1,0:T(2,128)} %face_match.1, bf16[2,512,256]{2,1,0:T(8,128)(2,1)} %vectors.1), custom_call_target="tpu_custom_call" | custom-call | tf_op jit(solution)/shard_map/pallas_call | solution.py:585
  174.5 2.3 %copy.7 = f32[2,512,256]{2,1,0:T(8,128)} copy(f32[2,512,256]{2,1,0:T(8,128)} %shard_map.55) | data formatting | bytes 2097152
where the time goes:
time: 177 us
  Pallas kernels  175 us (99%)
  local copies, waits for them, and re-layouts  2.26 us (1%)
    pallas_call x1, Pallas kernels, fused(): pl.pallas_call(functools.partial(assemble_and_filter, inner, ring), out_s...  175 us

commit v1 on v0

--- a/solution.py
+++ b/solution.py
@@ -133,14 +133,15 @@
     cross,
     nodal,
     faces,
-    after,
-    before,
+    turned,
     operator,
     own_sum,
     cross_sum,
     own_other,
     cross_other,
     state,
+    links,
+    edges,
     current,
     previous,
     local_sem,
@@ -150,8 +151,6 @@
     cross_recv,
     face_send,
     face_recv,
-    rim_send,
-    rim_recv,
     sum_send,
     sum_recv,
     block_send,
@@ -243,28 +242,16 @@
                 )
             )
 
-    def halo_copies(k, h, to_next, to_previous):
-        return (
-            send(
-                to_next,
-                state.at[k, h, pl.ds(0, total)],
-                halo_send.at[k, h, 0],
-                halo_recv.at[k, h, 0],
-                elem=following,
-            ),
-            send(
-                to_previous,
-                state.at[k, h, pl.ds((elements + 1) * total, total)],
-                halo_send.at[k, h, 1],
-                halo_recv.at[k, h, 1],
-                elem=preceding,
-            ),
-        )
-
-    for h in range(2):
-        piece = pl.ds(h * columns, columns)
-        for copy in halo_copies(0, h, vectors.at[elements - 1, :, piece], vectors.at[0, :, piece]):
-            copy.start()
+    low, high = pl.ds(0, 2 * faced), pl.ds(2 * faced, 2 * faced)
+
+    def halo(k, h, side):
+        return send(
+            edges.at[k, h, side],
+            links.at[k, h, 0, high] if side else links.at[k, h, elements - 1, low],
+            halo_send.at[k, h, side],
+            halo_recv.at[k, h, side],
+            elem=following if side else preceding,
+        )
 
     nodal_copy.wait()
     square = (faced, faced)
@@ -374,21 +361,33 @@
     for e in range(elements):
         face_copy(0, e, partner, partner).wait_recv()
         face_copy(2, e, diagonal_peer, partner).wait_recv()
-    right_cut, left_cut = pl.ds(0, 2 * faced), pl.ds(2 * faced, 2 * faced)
-    rims = (
-        send(
-            faces.at[0, :, left_cut], after, rim_send.at[0], rim_recv.at[0], elem=preceding
-        ),
-        send(
-            faces.at[elements - 1, :, right_cut],
-            before,
-            rim_send.at[1],
-            rim_recv.at[1],
-            elem=following,
-        ),
-    )
-    for copy in rims:
-        launch(copy)
+    for e in range(elements):
+        for index in range(4):
+            cut = faces[e, :, index * faced : (index + 1) * faced]
+            turn = index + 1 - 2 * (index % 2)
+            turned[e, turn * faced : (turn + 1) * faced, :] = cut.T
+
+    def coupled(e, cut, values):
+        found = jnp.dot(turned[e, cut, :], values, preferred_element_type=jnp.float32)
+        return (found * (1.0 / (4.0 * faced))).astype(jnp.bfloat16)
+
+    def edge(k, h, side, values):
+        edges[k, h, side] = coupled((elements - 1) * side, low if side else high, values)
+        launch(halo(k, h, side))
+
+    def inside(k, h, of):
+        for e in range(elements - 1):
+            links[k, h, e, low] = coupled(e + 1, high, of(e + 1))
+            links[k, h, e + 1, high] = coupled(e, low, of(e))
+
+    def given(h):
+        return lambda e: vectors[e, :, h * columns : (h + 1) * columns]
+
+    for h in range(2):
+        for side in range(2):
+            edge(0, h, side, given(h)((elements - 1) * side))
+    for h in range(2):
+        inside(0, h, given(h))
 
     def diagonal(e, to_chip):
         return product(
@@ -396,8 +395,7 @@
         ) / (4.0 * faced)
 
     def block_of(e, owner, to_chip):
-        offset = pl.multiple_of(total + to_chip * 2 * rows, 2 * rows)
-        return operator.at[e, aligned(owner, rows), pl.ds(offset, 2 * rows)]
+        return operator.at[e, aligned(owner, rows), aligned(to_chip, 2 * rows)]
 
     def block_copy(d, slot, owner, target):
         owner_chip = owner // 2
@@ -421,60 +419,28 @@
             launch(block_copy(d, e, me, peer))
     start_cross(parts - 1)
 
-    for copy in rims:
-        copy.wait_recv()
-
-    def between(target, left, right):
-        target[...] = (product(left, swapped(right)) / (4.0 * faced)).astype(jnp.bfloat16)
-
-    high = pl.ds(2 * total, total)
-    low = pl.ds(0, total)
-    for e in range(elements):
-        right_side = faces[e, :, right_cut]
-        left_side = faces[e, :, left_cut]
-        next_left = faces[e + 1, :, left_cut] if e + 1 < elements else after[...]
-        last_right = faces[e - 1, :, right_cut] if e else before[...]
-        between(operator.at[e, :, high], right_side, next_left)
-        between(operator.at[e, :, low], left_side, last_right)
-
     for h in range(2):
         for e in range(elements):
             piece = vectors[e, :, h * columns : (h + 1) * columns]
-            state[0, h, (e + 1) * total : (e + 2) * total] = piece
             current[h, e] = piece.astype(jnp.float32)
 
     norm = chebyshev_norm(STEPS)
     tile = min(total, 256)
     wide = 2 * rows
 
-    def halo_of(k, h):
-        return halo_copies(
-            k,
-            h,
-            state.at[k, h, pl.ds(elements * total, total)],
-            state.at[k, h, pl.ds(total, total)],
-        )
-
-    def halo_wait(k, h):
-        for copy in halo_of(k, h):
-            copy.wait()
-
-    def halo_start(k, h):
-        for copy in halo_of(k, h):
-            copy.start()
-
-    def times(k, h, e, some, begin, length):
+    def applied_by(e, some, begin, length, values):
         return jnp.dot(
             operator[e, some, begin : begin + length],
-            state[k, h, e * total + begin : e * total + begin + length],
+            values,
             preferred_element_type=jnp.float32,
         )
 
-    def rest(k, h, e, some, begin, length):
-        held = out[e, some, h * columns : (h + 1) * columns]
-        return held + times(k, h, e, some, begin, length)
-
-    def update(k, h, e, some, applied, first):
+    def through(k, h, e, some, cut):
+        return jnp.dot(
+            faces[e, some, cut], links[k, h, e, cut], preferred_element_type=jnp.float32
+        )
+
+    def update(k, h, e, some, applied):
         scale = (2.0 if k else 1.0) / HALF_WIDTH
         now = current[h, e, some]
         moved = scale * applied - (scale * CENTER) * now
@@ -485,8 +451,33 @@
         else:
             previous[h, e, some] = now
             current[h, e, some] = moved
-            target = pl.ds(pl.multiple_of((e + 1) * total + first, tile), tile)
-            state[k + 1, h, target] = moved.astype(jnp.bfloat16)
+            state[h, e, some] = moved.astype(jnp.bfloat16)
+
+    def before(k, h):
+        @pl.loop(0, total // tile)
+        def _(index):
+            some = pl.ds(pl.multiple_of(index * tile, tile), tile)
+            for e in range(elements):
+                found = applied_by(e, some, 0, total, state[h, e])
+                if e:
+                    found += through(k, h, e, some, high)
+                if e + 1 < elements:
+                    found += through(k, h, e, some, low)
+                out[e, some, h * columns : (h + 1) * columns] = found
+
+    def after(k, h, side):
+        e = (elements - 1) * (1 - side)
+        halo(k, h, side).wait_recv()
+
+        @pl.loop(0, total // tile)
+        def _(index):
+            some = pl.ds(pl.multiple_of(index * tile, tile), tile)
+            applied = out[e, some, h * columns : (h + 1) * columns]
+            applied += through(k, h, e, some, high if side else low)
+            update(k, h, e, some, applied)
+
+        if k + 1 < STEPS:
+            edge(k + 1, h, 1 - side, state[h, e])
 
     cross_face = diagonal(chip, far)
     cross_sum[...] = jnp.zeros(cross_sum.shape, jnp.float32)
@@ -499,15 +490,14 @@
                 block_copy(0, e, partner, partner).wait_recv()
                 block_copy(2, e, diagonal_peer, partner).wait_recv()
             for h in range(2):
-                halo_wait(0, h)
+                for side in range(2):
+                    halo(0, h, side).wait_recv()
+                held = pl.ds(h * columns, columns)
                 for e in range(elements):
                     for q in range(2):
                         some = slice(q * wide, (q + 1) * wide)
-                        held = pl.ds(h * columns, columns)
-                        out[e, some, held] = times(0, h, e, some, 0, total + (1 - q) * wide)
-                        out[e, some, held] += times(
-                            0, h, e, some, 2 * total - q * wide, total + q * wide
-                        )
+                        found = applied_by(e, some, q * wide, wide, vectors[e, some, held])
+                        out[e, some, held] = found + through(0, h, e, some, slice(0, 4 * faced))
         for other in range(2):
             side = lax.rem(core + other, 2)
             send(
@@ -537,39 +527,34 @@
         block_copy(d, elements, source, source).wait_recv()
     for e in range(elements):
         mine, theirs = e * wide, (1 - e) * wide
-        found = operator[e, mine : mine + wide, total + theirs : total + theirs + wide]
-        operator[e, theirs : theirs + wide, total + mine : total + mine + wide] = found.T
+        found = operator[e, mine : mine + wide, theirs : theirs + wide]
+        operator[e, theirs : theirs + wide, mine : mine + wide] = found.T
 
     for h in range(2):
-        for q in range(2):
-            some = slice(q * wide, (q + 1) * wide)
-            begin = total + (1 - q) * wide
-            for e in range(elements):
-                update(0, h, e, some, rest(0, h, e, some, begin, wide), q * wide)
-        halo_start(1, h)
+        held = pl.ds(h * columns, columns)
+        for side in (1, 0):
+            e = (elements - 1) * (1 - side)
+            for q in range(2):
+                some = slice(q * wide, (q + 1) * wide)
+                rest = slice((1 - q) * wide, (2 - q) * wide)
+                applied = out[e, some, held]
+                applied += applied_by(e, some, (1 - q) * wide, wide, vectors[e, rest, held])
+                update(0, h, e, some, applied)
+            edge(1, h, 1 - side, state[h, e])
+
+    def kept(h):
+        return lambda e: state[h, e]
+
+    for h in range(2):
+        inside(1, h, kept(h))
+        before(1, h)
     for k in range(1, STEPS):
         for h in range(2):
-
-            @pl.loop(0, total // tile)
-            def _(index, k=k, h=h):
-                some = pl.ds(pl.multiple_of(index * tile, tile), tile)
-                for e in range(elements):
-                    out[e, some, h * columns : (h + 1) * columns] = times(
-                        k, h, e, some, 0 if e else total, 2 * total
-                    )
-
-            halo_wait(k, h)
-
-            @pl.loop(0, total // tile)
-            def _(index, k=k, h=h):
-                first = pl.multiple_of(index * tile, tile)
-                some = pl.ds(first, tile)
-                for e in range(elements):
-                    applied = rest(k, h, e, some, 2 * total if e else 0, total)
-                    update(k, h, e, some, applied, first)
-
+            for side in (1, 0):
+                after(k, h, side)
             if k + 1 < STEPS:
-                halo_start(k + 1, h)
+                inside(k + 1, h, kept(h))
+                before(k + 1, h)
 
     for copy in sends:
         copy.wait_send()
@@ -592,14 +577,15 @@
             pltpu.VMEM((parts, 2 * rows, half), bf16),
             pltpu.VMEM((elements, 2, rows, grid), bf16),
             pltpu.VMEM((elements, total, 4 * faced), bf16),
-            pltpu.VMEM((total, 2 * faced), bf16),
-            pltpu.VMEM((total, 2 * faced), bf16),
-            pltpu.VMEM((elements, total, 3 * total), bf16),
+            pltpu.VMEM((elements, 4 * faced, total), bf16),
+            pltpu.VMEM((elements, total, total), bf16),
             pltpu.VMEM((elements, 2 * rows, 2 * rows), f32),
             pltpu.VMEM((2 * rows, 2 * rows), f32),
             pltpu.VMEM((elements, rows, 2 * rows), f32),
             pltpu.VMEM((rows, 2 * rows), f32),
-            pltpu.VMEM((STEPS, 2, (elements + 2) * total, width // 2), bf16),
+            pltpu.VMEM((2, elements, total, width // 2), bf16),
+            pltpu.VMEM((STEPS, 2, elements, 4 * faced, width // 2), bf16),
+            pltpu.VMEM((STEPS, 2, 2, 2 * faced, width // 2), bf16),
             pltpu.VMEM((2, elements, total, width // 2), f32),
             pltpu.VMEM((2, elements, total, width // 2), f32),
             dma((1 + elements, parts)),
@@ -609,8 +595,6 @@
             dma((2, parts)),
             dma((inner - 1, elements)),
             dma((inner - 1, elements)),
-            dma((2,)),
-            dma((2,)),
             dma((elements + 1,)),
             dma((elements + 1,)),
             dma((inner - 1, elements + 1)),

time: 177 us -> 154 us (0.87)
  Pallas kernels: 175 us -> 152 us
    pallas_call x1, Pallas kernels: 175 us -> 152 us  [fused(): pl.pallas_call(functools.partial(assemble_and_filter, inner, ring), out_s...]
where the time goes in v1:
time: 154 us
  Pallas kernels  152 us (99%)
  local copies, waits for them, and re-layouts  2.26 us (1%)
    pallas_call x1, Pallas kernels, fused(): pl.pallas_call(functools.partial(assemble_and_filter, inner, ring), out_s...  152 us

profile of v1, /device:TPU:0, one launch (start us, length us, event | category | flops | bytes accessed | tf_op | source)
XLA Modules:
  0.0 154.3 jit_solution(15936718221033494327)
XLA Ops:
  0.0 152.0 %shard_map.55 = f32[2,512,256]{2,1,0:T(8,128)} custom-call(bf16[2,4,128,4096]{3,2,1,0:T(8,128)(2,1)} %basis.1, f32[2,4096]{1,0:T(2,128)} %potential.1, s32[2,2,128]{2,1,0:T(2,128)} %face_index.1, s32[2,128]{1,0:T(2,128)} %face_match.1, bf16[2,512,256]{2,1,0:T(8,128)(2,1)} %vectors.1), custom_call_target="tpu_custom_call" | custom-call | tf_op jit(solution)/shard_map/pallas_call | solution.py:570
  152.1 2.3 %copy.7 = f32[2,512,256]{2,1,0:T(8,128)} copy(f32[2,512,256]{2,1,0:T(8,128)} %shard_map.55) | data formatting | bytes 2097152

commit v2 on v1

--- a/solution.py
+++ b/solution.py
@@ -243,14 +243,15 @@
             )
 
     low, high = pl.ds(0, 2 * faced), pl.ds(2 * faced, 2 * faced)
+    turn_side = lax.rem(place, 2)
 
     def halo(k, h, side):
         return send(
             edges.at[k, h, side],
-            links.at[k, h, 0, high] if side else links.at[k, h, elements - 1, low],
+            links.at[k, h, (elements - 1) * (1 - side), aligned(side, 2 * faced)],
             halo_send.at[k, h, side],
             halo_recv.at[k, h, side],
-            elem=following if side else preceding,
+            elem=lax.rem(place + ring + 2 * side - 1, ring),
         )
 
     nodal_copy.wait()
@@ -372,8 +373,7 @@
         return (found * (1.0 / (4.0 * faced))).astype(jnp.bfloat16)
 
     def edge(k, h, side, values):
-        edges[k, h, side] = coupled((elements - 1) * side, low if side else high, values)
-        launch(halo(k, h, side))
+        edges[k, h, side] = coupled((elements - 1) * side, aligned(1 - side, 2 * faced), values)
 
     def inside(k, h, of):
         for e in range(elements - 1):
@@ -386,6 +386,7 @@
     for h in range(2):
         for side in range(2):
             edge(0, h, side, given(h)((elements - 1) * side))
+            launch(halo(0, h, side))
     for h in range(2):
         inside(0, h, given(h))
 
@@ -473,11 +474,15 @@
         def _(index):
             some = pl.ds(pl.multiple_of(index * tile, tile), tile)
             applied = out[e, some, h * columns : (h + 1) * columns]
-            applied += through(k, h, e, some, high if side else low)
+            applied += through(k, h, e, some, aligned(side, 2 * faced))
             update(k, h, e, some, applied)
 
         if k + 1 < STEPS:
             edge(k + 1, h, 1 - side, state[h, e])
+
+    def fire(k, h):
+        for side in (turn_side, 1 - turn_side):
+            launch(halo(k, h, side))
 
     cross_face = diagonal(chip, far)
     cross_sum[...] = jnp.zeros(cross_sum.shape, jnp.float32)
@@ -541,6 +546,7 @@
                 applied += applied_by(e, some, (1 - q) * wide, wide, vectors[e, rest, held])
                 update(0, h, e, some, applied)
             edge(1, h, 1 - side, state[h, e])
+        fire(1, h)
 
     def kept(h):
         return lambda e: state[h, e]
@@ -550,8 +556,10 @@
         before(1, h)
     for k in range(1, STEPS):
         for h in range(2):
-            for side in (1, 0):
+            for side in (1 - turn_side, turn_side):
                 after(k, h, side)
+                if k + 1 < STEPS:
+                    launch(halo(k + 1, h, 1 - side))
             if k + 1 < STEPS:
                 inside(k + 1, h, kept(h))
                 before(k + 1, h)
@@ -569,7 +577,7 @@
     vmem = pl.BlockSpec(memory_space=pltpu.VMEM)
     return pl.pallas_call(
         functools.partial(assemble_and_filter, inner, ring),
-        out_shape=jax.ShapeDtypeStruct(vectors.shape, f32),
+        out_shape=pltpu.VMEM(vectors.shape, f32),
         in_specs=[pl.BlockSpec(memory_space=pltpu.HBM)] + [vmem] * 4,
         out_specs=vmem,
         scratch_shapes=[

time: 154 us -> 148 us (0.961)
  Pallas kernels: 152 us -> 147 us
    pallas_call x1, Pallas kernels: 152 us -> 147 us  [fused(): pl.pallas_call(functools.partial(assemble_and_filter, inner, ring), out_s...]
where the time goes in v2:
time: 148 us
  Pallas kernels  147 us (99%)
    pallas_call x1, Pallas kernels, fused(): pl.pallas_call(functools.partial(assemble_and_filter, inner, ring), out_s...  147 us

profile of v2, /device:TPU:0, one launch (start us, length us, event | category | flops | bytes accessed | tf_op | source)
XLA Modules:
  0.0 148.1 jit_solution(1441250922582303365)
XLA Ops:
  0.0 147.1 %shard_map.55 = f32[2,512,256]{2,1,0:T(8,128)S(1)} custom-call(bf16[2,4,128,4096]{3,2,1,0:T(8,128)(2,1)} %basis.1, f32[2,4096]{1,0:T(2,128)} %potential.1, s32[2,2,128]{2,1,0:T(2,128)} %face_index.1, s32[2,128]{1,0:T(2,128)} %face_match.1, bf16[2,512,256]{2,1,0:T(8,128)(2,1)} %vectors.1), custom_call_target="tpu_custom_call" | custom-call | tf_op jit(solution)/shard_map/pallas_call | solution.py:578
  147.1 1.0 copy.7

commit v3 on v2

--- a/solution.py
+++ b/solution.py
@@ -124,11 +124,18 @@
     inner,
     ring,
     basis,
+    potential_in,
+    face_index_in,
+    face_match_in,
+    vectors_in,
+    out,
     potential,
     face_index,
     face_match,
     vectors,
-    out,
+    found,
+    found_mine,
+    found_other,
     own,
     cross,
     nodal,
@@ -137,6 +144,7 @@
     operator,
     own_sum,
     cross_sum,
+    cross_face,
     own_other,
     cross_other,
     state,
@@ -144,6 +152,7 @@
     edges,
     current,
     previous,
+    input_sem,
     local_sem,
     pair_send,
     pair_recv,
@@ -190,6 +199,9 @@
             device_id_type=MESH,
         )
 
+    pieces = [(k, 0, half) for k in range(parts - 1)]
+    pieces += [(parts - 1, begin, step_k) for begin in range(0, half, step_k)]
+
     barrier = pltpu.get_barrier_semaphore()
     for peer in peers:
         pl.semaphore_signal(barrier, inc=1, device_id={"inner": peer}, device_id_type=MESH)
@@ -198,6 +210,19 @@
 
     nodal_copy = pltpu.make_async_copy(basis.at[:, 0:2], nodal, local_sem.at[0, 0])
     nodal_copy.start()
+    moved_in = [
+        pltpu.make_async_copy(source, target, input_sem.at[index])
+        for index, (source, target) in enumerate(
+            (
+                (potential_in, potential),
+                (face_index_in, face_index),
+                (face_match_in, face_match),
+                (vectors_in, vectors),
+            )
+        )
+    ]
+    for copy in moved_in:
+        copy.start()
     local = {}
     for e in range(elements):
         for k in range(parts):
@@ -216,18 +241,34 @@
         copy.start()
         sends.append(copy)
 
-    def start_cross(k):
+    def cross_copy(piece, other):
+        k, begin, size = pieces[piece]
+        side = lax.rem(core + other, 2)
+        return send(
+            basis.at[far, k, :, pl.ds(pl.multiple_of(side * half + begin, step_k), size)],
+            cross.at[k, aligned(core, rows), begin : begin + size],
+            cross_send.at[other, piece],
+            cross_recv.at[other, piece],
+            inner=far * 2 + side,
+        )
+
+    def cross_wait(piece):
+        k, begin, size = pieces[piece]
         for other in range(2):
             side = lax.rem(core + other, 2)
-            launch(
-                send(
-                    basis.at[far, k, :, aligned(side, half)],
-                    cross.at[k, aligned(core, rows)],
-                    cross_send.at[other, k],
-                    cross_recv.at[other, k],
-                    inner=far * 2 + side,
-                )
-            )
+            send(
+                basis.at[far, k, :, pl.ds(pl.multiple_of(core * half + begin, step_k), size)],
+                cross.at[k, aligned(side, rows), begin : begin + size],
+                cross_send.at[other, piece],
+                cross_recv.at[other, piece],
+                inner=far * 2 + side,
+            ).wait_recv()
+
+    def start_cross(wanted):
+        for piece, (k, _, _) in enumerate(pieces):
+            if k == wanted:
+                for other in range(2):
+                    launch(cross_copy(piece, other))
 
     start_cross(0)
     for e in range(elements):
@@ -254,26 +295,47 @@
             elem=lax.rem(place + ring + 2 * side - 1, ring),
         )
 
+    for copy in moved_in:
+        copy.wait()
     nodal_copy.wait()
-    square = (faced, faced)
-    for e in range(elements):
+
+    def points_of(e):
+        square = (faced, faced)
         down = lax.broadcasted_iota(jnp.int32, square, 0)
         along = lax.broadcasted_iota(jnp.int32, square, 1)
         left_row = jnp.broadcast_to(face_index[e, 0:1, :], square)
         left_column = jnp.sum(jnp.where(down == along, left_row, 0), axis=1, keepdims=True)
-        matched = jnp.broadcast_to(face_match[e : e + 1, :], square) == down
+        matched = jnp.broadcast_to(face_match[pl.ds(e, 1), :], square) == down
         left_points = jnp.sum(
             jnp.where(matched, jnp.broadcast_to(left_column, square), 0), axis=0, keepdims=True
         )
-        points = jnp.concatenate([face_index[e, 1:2, :], left_points], axis=1)
-
-        def pick(index, found, e=e, points=points):
+        return jnp.concatenate([face_index[e, 1:2, :], left_points], axis=1)
+
+    def chosen_at(points, offset):
+        spots = lax.broadcasted_iota(jnp.int32, (step_k, 2 * faced), 0) + offset
+        chosen = (spots == jnp.broadcast_to(points, spots.shape)).astype(jnp.float32)
+        return chosen.astype(jnp.bfloat16)
+
+    def write_faces(e, where, value, slope):
+        right_value, left_value = value[:, :faced], value[:, faced:]
+        right_slope, left_slope = slope[:, :faced], slope[:, faced:]
+        sides = (
+            0.5 * right_value - 0.25 * right_slope,
+            right_value,
+            -0.5 * left_value - 0.25 * left_slope,
+            -left_value,
+        )
+        for index, side in enumerate(sides):
+            faces[e, where, index * faced : (index + 1) * faced] = side.astype(jnp.bfloat16)
+
+    for e in range(elements):
+        points = points_of(e)
+
+        def pick(index, values, e=e, points=points):
             offset = pl.multiple_of(index * step_k, step_k)
-            spots = lax.broadcasted_iota(jnp.int32, (step_k, 2 * faced), 0) + offset
-            chosen = (spots == jnp.broadcast_to(points, spots.shape)).astype(jnp.float32)
-            chosen = chosen.astype(jnp.bfloat16)
+            chosen = chosen_at(points, offset)
             return tuple(
-                found[k]
+                values[k]
                 + jnp.dot(
                     nodal[e, k, :, pl.ds(offset, step_k)],
                     chosen,
@@ -284,24 +346,15 @@
 
         start = jnp.zeros((rows, 2 * faced), jnp.float32)
         value, slope = lax.fori_loop(0, grid // step_k, pick, (start, start))
-        right_value, left_value = value[:, :faced], value[:, faced:]
-        right_slope, left_slope = slope[:, :faced], slope[:, faced:]
-        mine = aligned(me, rows)
-        pieces = (
-            0.5 * right_value - 0.25 * right_slope,
-            right_value,
-            -0.5 * left_value - 0.25 * left_slope,
-            -left_value,
-        )
-        for index, piece in enumerate(pieces):
-            faces[e, mine, index * faced : (index + 1) * faced] = piece.astype(jnp.bfloat16)
-    def face_copy(d, e, owner, target):
+        write_faces(e, aligned(me, rows), value, slope)
+
+    def face_copy(d, slot, e, owner, target):
         block = faces.at[e, aligned(owner, rows)]
-        return send(block, block, face_send.at[d, e], face_recv.at[d, e], inner=target)
-
-    for d, peer in routes:
-        for e in range(elements):
-            launch(face_copy(d, e, me, peer))
+        return send(block, block, face_send.at[d, slot], face_recv.at[d, slot], inner=target)
+
+    for e in range(elements):
+        launch(face_copy(0, e, e, me, partner))
+    launch(face_copy(1, 0, chip, me, across))
     for k in range(1, parts - 1):
         start_cross(k)
 
@@ -315,10 +368,10 @@
         order = [k + 1 - 2 * (k % 2) for k in range(len(cut))]
         return jnp.concatenate([cut[k] for k in order], axis=1)
 
-    def weighted(row_left, row_right, left, right, k, target, scale_left):
-        @pl.loop(0, half // step_k)
+    def weighted(row_left, row_right, left, right, k, target, scale_left, begin=0, size=half):
+        @pl.loop(0, size // step_k)
         def _(index):
-            offset = pl.multiple_of(index * step_k, step_k)
+            offset = pl.multiple_of(begin + index * step_k, step_k)
             span = pl.ds(offset, step_k)
             there = pl.ds(pl.multiple_of(core * half + offset, step_k), step_k)
             one = left[:, span]
@@ -357,38 +410,7 @@
         )
 
     for e in range(elements):
-        face_copy(1, e, across, across).wait_recv()
-        launch(face_copy(2, e, across, partner))
-    for e in range(elements):
-        face_copy(0, e, partner, partner).wait_recv()
-        face_copy(2, e, diagonal_peer, partner).wait_recv()
-    for e in range(elements):
-        for index in range(4):
-            cut = faces[e, :, index * faced : (index + 1) * faced]
-            turn = index + 1 - 2 * (index % 2)
-            turned[e, turn * faced : (turn + 1) * faced, :] = cut.T
-
-    def coupled(e, cut, values):
-        found = jnp.dot(turned[e, cut, :], values, preferred_element_type=jnp.float32)
-        return (found * (1.0 / (4.0 * faced))).astype(jnp.bfloat16)
-
-    def edge(k, h, side, values):
-        edges[k, h, side] = coupled((elements - 1) * side, aligned(1 - side, 2 * faced), values)
-
-    def inside(k, h, of):
-        for e in range(elements - 1):
-            links[k, h, e, low] = coupled(e + 1, high, of(e + 1))
-            links[k, h, e + 1, high] = coupled(e, low, of(e))
-
-    def given(h):
-        return lambda e: vectors[e, :, h * columns : (h + 1) * columns]
-
-    for h in range(2):
-        for side in range(2):
-            edge(0, h, side, given(h)((elements - 1) * side))
-            launch(halo(0, h, side))
-    for h in range(2):
-        inside(0, h, given(h))
+        face_copy(0, e, e, partner, partner).wait_recv()
 
     def diagonal(e, to_chip):
         return product(
@@ -480,41 +502,95 @@
         if k + 1 < STEPS:
             edge(k + 1, h, 1 - side, state[h, e])
 
-    def fire(k, h):
-        for side in (turn_side, 1 - turn_side):
-            launch(halo(k, h, side))
-
-    cross_face = diagonal(chip, far)
+    def coupled(e, cut, values):
+        found = jnp.dot(turned[e, cut, :], values, preferred_element_type=jnp.float32)
+        return (found * (1.0 / (4.0 * faced))).astype(jnp.bfloat16)
+
+    def edge(k, h, side, values):
+        edges[k, h, side] = coupled((elements - 1) * side, aligned(1 - side, 2 * faced), values)
+
+    def inside(k, h, of):
+        for e in range(elements - 1):
+            links[k, h, e, low] = coupled(e + 1, high, of(e + 1))
+            links[k, h, e + 1, high] = coupled(e, low, of(e))
+
+    def given(h):
+        return lambda e: vectors[e, :, h * columns : (h + 1) * columns]
+
+    def far_faces():
+        points = points_of(chip)
+        found[...] = jnp.zeros(found.shape, jnp.float32)
+
+        @pl.loop(0, half // step_k)
+        def _(index):
+            offset = pl.multiple_of(index * step_k, step_k)
+            chosen = chosen_at(points, core * half + offset)
+            for k in range(2):
+                found[k] += jnp.dot(
+                    cross[k, :, pl.ds(offset, step_k)],
+                    chosen,
+                    preferred_element_type=jnp.float32,
+                )
+
+        found_mine[...] = found[...].astype(jnp.bfloat16)
+        swap = send(
+            found_mine, found_other, face_send.at[1, 1], face_recv.at[1, 1], inner=partner
+        )
+        launch(swap)
+        face_copy(1, 0, far, across, across).wait_recv()
+        launch(face_copy(2, 0, far, across, partner))
+        swap.wait_recv()
+        value, slope = (found[k] + found_other[k].astype(jnp.float32) for k in range(2))
+        write_faces(chip, aligned(far, 2 * rows), value, slope)
+        face_copy(2, 0, far, diagonal_peer, partner).wait_recv()
+
+    def first_partial():
+        for e in range(elements):
+            block_copy(1, e, across, across).wait_recv()
+            launch(block_copy(2, e, across, partner))
+        for e in range(elements):
+            block_copy(0, e, partner, partner).wait_recv()
+            block_copy(2, e, diagonal_peer, partner).wait_recv()
+        for h in range(2):
+            for side in range(2):
+                halo(0, h, side).wait_recv()
+            held = pl.ds(h * columns, columns)
+            for e in range(elements):
+                for q in range(2):
+                    some = slice(q * wide, (q + 1) * wide)
+                    value = applied_by(e, some, q * wide, wide, vectors[e, some, held])
+                    out[e, some, held] = value + through(0, h, e, some, slice(0, 4 * faced))
+
     cross_sum[...] = jnp.zeros(cross_sum.shape, jnp.float32)
-    for k in range(parts):
-        if k + 1 == parts:
+    for piece, (k, begin, size) in enumerate(pieces):
+        if k + 1 == parts and not begin:
+            first_partial()
+        cross_wait(piece)
+        weighted(
+            pl.ds(chip, 1),
+            pl.ds(chip, 1),
+            own.at[chip, k],
+            cross.at[k],
+            k,
+            cross_sum,
+            False,
+            begin,
+            size,
+        )
+        if k == 1:
+            far_faces()
             for e in range(elements):
-                block_copy(1, e, across, across).wait_recv()
-                launch(block_copy(2, e, across, partner))
-            for e in range(elements):
-                block_copy(0, e, partner, partner).wait_recv()
-                block_copy(2, e, diagonal_peer, partner).wait_recv()
+                for index in range(4):
+                    cut = faces[e, :, index * faced : (index + 1) * faced]
+                    turn = index + 1 - 2 * (index % 2)
+                    turned[e, turn * faced : (turn + 1) * faced, :] = cut.T
             for h in range(2):
                 for side in range(2):
-                    halo(0, h, side).wait_recv()
-                held = pl.ds(h * columns, columns)
-                for e in range(elements):
-                    for q in range(2):
-                        some = slice(q * wide, (q + 1) * wide)
-                        found = applied_by(e, some, q * wide, wide, vectors[e, some, held])
-                        out[e, some, held] = found + through(0, h, e, some, slice(0, 4 * faced))
-        for other in range(2):
-            side = lax.rem(core + other, 2)
-            send(
-                basis.at[far, k, :, aligned(core, half)],
-                cross.at[k, aligned(side, rows)],
-                cross_send.at[other, k],
-                cross_recv.at[other, k],
-                inner=far * 2 + side,
-            ).wait_recv()
-        weighted(
-            pl.ds(chip, 1), pl.ds(chip, 1), own.at[chip, k], cross.at[k], k, cross_sum, False
-        )
+                    edge(0, h, side, given(h)((elements - 1) * side))
+                    launch(halo(0, h, side))
+            for h in range(2):
+                inside(0, h, given(h))
+            cross_face[...] = diagonal(chip, far)
     final = send(
         cross_sum.at[aligned(1 - core, rows)],
         cross_other,
@@ -525,28 +601,29 @@
     launch(final)
     final.wait_recv()
     gram = (cross_sum[aligned(core, rows)] + cross_other[...]) / grid
-    block_of(chip, me, far)[...] = (gram + cross_face).astype(jnp.bfloat16)
-    for d, peer in enumerate(sources):
-        launch(block_copy(d, elements, me, peer))
-    for d, source in enumerate(sources):
-        block_copy(d, elements, source, source).wait_recv()
-    for e in range(elements):
-        mine, theirs = e * wide, (1 - e) * wide
-        found = operator[e, mine : mine + wide, theirs : theirs + wide]
-        operator[e, theirs : theirs + wide, mine : mine + wide] = found.T
-
-    for h in range(2):
-        held = pl.ds(h * columns, columns)
-        for side in (1, 0):
-            e = (elements - 1) * (1 - side)
+    block_of(chip, me, far)[...] = (gram + cross_face[...]).astype(jnp.bfloat16)
+    for d in (1, 2, 0):
+        launch(block_copy(d, elements, me, sources[d]))
+
+    def finish(e):
+        mine, theirs = aligned(e, wide), aligned(1 - e, wide)
+        operator[e, theirs, mine] = operator[e, mine, theirs].T
+        for h in range(2):
+            held = pl.ds(h * columns, columns)
             for q in range(2):
                 some = slice(q * wide, (q + 1) * wide)
                 rest = slice((1 - q) * wide, (2 - q) * wide)
                 applied = out[e, some, held]
                 applied += applied_by(e, some, (1 - q) * wide, wide, vectors[e, rest, held])
                 update(0, h, e, some, applied)
-            edge(1, h, 1 - side, state[h, e])
-        fire(1, h)
+            edge(1, h, e, state[h, e])
+            launch(halo(1, h, e))
+
+    block_copy(0, elements, partner, partner).wait_recv()
+    finish(chip)
+    for d in (1, 2):
+        block_copy(d, elements, sources[d], sources[d]).wait_recv()
+    finish(far)
 
     def kept(h):
         return lambda e: state[h, e]
@@ -573,14 +650,22 @@
     total, width = vectors.shape[1], vectors.shape[2]
     faced = face_index.shape[2]
     half = grid // 2
+    pieces = parts - 1 + half // min(half, 512)
     bf16, f32, dma = jnp.bfloat16, jnp.float32, pltpu.SemaphoreType.DMA
     vmem = pl.BlockSpec(memory_space=pltpu.VMEM)
     return pl.pallas_call(
         functools.partial(assemble_and_filter, inner, ring),
         out_shape=pltpu.VMEM(vectors.shape, f32),
-        in_specs=[pl.BlockSpec(memory_space=pltpu.HBM)] + [vmem] * 4,
+        in_specs=[pl.BlockSpec(memory_space=pltpu.HBM)] * 5,
         out_specs=vmem,
         scratch_shapes=[
+            pltpu.VMEM(potential.shape, f32),
+            pltpu.VMEM(face_index.shape, jnp.int32),
+            pltpu.VMEM(face_match.shape, jnp.int32),
+            pltpu.VMEM(vectors.shape, bf16),
+            pltpu.VMEM((2, 2 * rows, 2 * faced), f32),
+            pltpu.VMEM((2, 2 * rows, 2 * faced), bf16),
+            pltpu.VMEM((2, 2 * rows, 2 * faced), bf16),
             pltpu.VMEM((elements, parts, 2 * rows, half), bf16),
             pltpu.VMEM((parts, 2 * rows, half), bf16),
             pltpu.VMEM((elements, 2, rows, grid), bf16),
@@ -589,6 +674,7 @@
             pltpu.VMEM((elements, total, total), bf16),
             pltpu.VMEM((elements, 2 * rows, 2 * rows), f32),
             pltpu.VMEM((2 * rows, 2 * rows), f32),
+            pltpu.VMEM((rows, 2 * rows), f32),
             pltpu.VMEM((elements, rows, 2 * rows), f32),
             pltpu.VMEM((rows, 2 * rows), f32),
             pltpu.VMEM((2, elements, total, width // 2), bf16),
@@ -596,11 +682,12 @@
             pltpu.VMEM((STEPS, 2, 2, 2 * faced, width // 2), bf16),
             pltpu.VMEM((2, elements, total, width // 2), f32),
             pltpu.VMEM((2, elements, total, width // 2), f32),
+            dma((4,)),
             dma((1 + elements, parts)),
             dma((elements, parts)),
             dma((elements, parts)),
-            dma((2, parts)),
-            dma((2, parts)),
+            dma((2, pieces)),
+            dma((2, pieces)),
             dma((inner - 1, elements)),
             dma((inner - 1, elements)),
             dma((elements + 1,)),

time: 148 us -> 144 us (0.973)
  Pallas kernels: 147 us -> 143 us
    pallas_call x1, Pallas kernels: 147 us -> 143 us  [fused(): pl.pallas_call(functools.partial(assemble_and_filter, inner, ring), out_s...]
where the time goes in v3:
time: 144 us
  Pallas kernels  143 us (99%)
    pallas_call x1, Pallas kernels, fused(): pl.pallas_call(functools.partial(assemble_and_filter, inner, ring), out_s...  143 us

profile of v3, /device:TPU:0, one launch (start us, length us, event | category | flops | bytes accessed | tf_op | source)
XLA Modules:
  0.0 143.6 jit_solution(14574682490633288893)
XLA Ops:
  0.0 142.6 %shard_map.55 = f32[2,512,256]{2,1,0:T(8,128)S(1)} custom-call(bf16[2,4,128,4096]{3,2,1,0:T(8,128)(2,1)} %basis.1, f32[2,4096]{1,0:T(2,128)} %potential_in.1, s32[2,2,128]{2,1,0:T(2,128)} %face_index_in.1, s32[2,128]{1,0:T(2,128)} %face_match_in.1, bf16[2,512,256]{2,1,0:T(8,128)(2,1)} %vectors_in.1), custom_call_target="tpu_custom_call" | custom-call | tf_op jit(solution)/shard_map/pallas_call | solution.py:656
  142.6 1.0 copy.7

commit v4 on v3

--- a/solution.py
+++ b/solution.py
@@ -166,6 +166,7 @@
     block_recv,
     halo_send,
     halo_recv,
+    token,
 ):
     elements, parts, rows, grid = basis.shape
     total = rows * inner
@@ -178,8 +179,6 @@
     chip, core = me // 2, lax.rem(me, 2)
     partner = chip * 2 + (1 - core)
     far = 1 - chip
-    following = lax.rem(place + 1, ring)
-    preceding = lax.rem(place + ring - 1, ring)
     peers = [lax.rem(me + d, inner) for d in range(1, inner)]
     across = far * 2 + core
     diagonal_peer = far * 2 + (1 - core)
@@ -205,8 +204,19 @@
     barrier = pltpu.get_barrier_semaphore()
     for peer in peers:
         pl.semaphore_signal(barrier, inc=1, device_id={"inner": peer}, device_id_type=MESH)
-    for peer in (preceding, following):
-        pl.semaphore_signal(barrier, inc=1, device_id={"elem": peer}, device_id_type=MESH)
+    odd, level = lax.rem(place, 2), lax.div(place, 2)
+    top = lax.div(level, ring // 2 - 1)
+    later = place + (1 - odd) * (2 - top) - 2 * odd
+    earlier = place + odd * (2 - 3 * top) - 2 * (1 - odd)
+
+    @pl.when(place != 1)
+    def _():
+        pl.semaphore_signal(barrier, inc=1, device_id={"elem": later}, device_id_type=MESH)
+
+    @pl.when(place != 0)
+    def _():
+        pl.semaphore_signal(barrier, inc=1, device_id={"elem": earlier}, device_id_type=MESH)
+
 
     nodal_copy = pltpu.make_async_copy(basis.at[:, 0:2], nodal, local_sem.at[0, 0])
     nodal_copy.start()
@@ -233,7 +243,7 @@
             )
             local[e, k].start()
 
-    pl.semaphore_wait(barrier, inner + 1)
+    pl.semaphore_wait(barrier, inner + lax.div(place + ring - 2, ring))
 
     sends = []
 
@@ -289,7 +299,12 @@
     def halo(k, h, side):
         return send(
             edges.at[k, h, side],
-            links.at[k, h, (elements - 1) * (1 - side), aligned(side, 2 * faced)],
+            links.at[
+                k,
+                (elements - 1) * (1 - side),
+                aligned(side, 2 * faced),
+                h * columns : (h + 1) * columns,
+            ],
             halo_send.at[k, h, side],
             halo_recv.at[k, h, side],
             elem=lax.rem(place + ring + 2 * side - 1, ring),
@@ -442,10 +457,22 @@
             launch(block_copy(d, e, me, peer))
     start_cross(parts - 1)
 
-    for h in range(2):
-        for e in range(elements):
-            piece = vectors[e, :, h * columns : (h + 1) * columns]
-            current[h, e] = piece.astype(jnp.float32)
+    def pass_on(index, comes, goes, target):
+        @pl.when(comes)
+        def _():
+            pl.semaphore_wait(token.at[index], 1)
+
+        @pl.when(goes)
+        def _():
+            pl.semaphore_signal(
+                token.at[index], inc=1, device_id={"elem": target}, device_id_type=MESH
+            )
+
+    pass_on(0, place != 0, place != 1, later)
+    pass_on(1, place != 1, place != 0, earlier)
+
+    for e in range(elements):
+        current[e] = vectors[e].astype(jnp.float32)
 
     norm = chebyshev_norm(STEPS)
     tile = min(total, 256)
@@ -458,64 +485,67 @@
             preferred_element_type=jnp.float32,
         )
 
-    def through(k, h, e, some, cut):
+    def through(k, e, some, cut, held):
         return jnp.dot(
-            faces[e, some, cut], links[k, h, e, cut], preferred_element_type=jnp.float32
-        )
-
-    def update(k, h, e, some, applied):
+            faces[e, some, cut], links[k, e, cut, held], preferred_element_type=jnp.float32
+        )
+
+    def update(k, e, some, held, applied):
         scale = (2.0 if k else 1.0) / HALF_WIDTH
-        now = current[h, e, some]
+        now = current[e, some, held]
         moved = scale * applied - (scale * CENTER) * now
         if k:
-            moved = moved - previous[h, e, some]
+            moved = moved - previous[e, some, held]
         if k + 1 == STEPS:
-            out[e, some, h * columns : (h + 1) * columns] = moved * (1.0 / norm)
+            out[e, some, held] = moved * (1.0 / norm)
         else:
-            previous[h, e, some] = now
-            current[h, e, some] = moved
-            state[h, e, some] = moved.astype(jnp.bfloat16)
-
-    def before(k, h):
+            previous[e, some, held] = now
+            current[e, some, held] = moved
+            state[e, some, held] = moved.astype(jnp.bfloat16)
+
+    def coupled(e, cut, values):
+        value = jnp.dot(turned[e, cut, :], values, preferred_element_type=jnp.float32)
+        return (value * (1.0 / (4.0 * faced))).astype(jnp.bfloat16)
+
+    def inside(k, of):
+        for e in range(elements - 1):
+            links[k, e, low] = coupled(e + 1, high, of[e + 1])
+            links[k, e + 1, high] = coupled(e, low, of[e])
+
+    def before(k):
         @pl.loop(0, total // tile)
         def _(index):
             some = pl.ds(pl.multiple_of(index * tile, tile), tile)
             for e in range(elements):
-                found = applied_by(e, some, 0, total, state[h, e])
+                value = applied_by(e, some, 0, total, state[e])
                 if e:
-                    found += through(k, h, e, some, high)
+                    value += through(k, e, some, high, slice(None))
                 if e + 1 < elements:
-                    found += through(k, h, e, some, low)
-                out[e, some, h * columns : (h + 1) * columns] = found
+                    value += through(k, e, some, low, slice(None))
+                out[e, some] = value
 
     def after(k, h, side):
         e = (elements - 1) * (1 - side)
+        held = slice(h * columns, (h + 1) * columns)
         halo(k, h, side).wait_recv()
 
         @pl.loop(0, total // tile)
         def _(index):
             some = pl.ds(pl.multiple_of(index * tile, tile), tile)
-            applied = out[e, some, h * columns : (h + 1) * columns]
-            applied += through(k, h, e, some, aligned(side, 2 * faced))
-            update(k, h, e, some, applied)
+            applied = out[e, some, held]
+            applied += through(k, e, some, aligned(side, 2 * faced), held)
+            update(k, e, some, held, applied)
 
         if k + 1 < STEPS:
-            edge(k + 1, h, 1 - side, state[h, e])
-
-    def coupled(e, cut, values):
-        found = jnp.dot(turned[e, cut, :], values, preferred_element_type=jnp.float32)
-        return (found * (1.0 / (4.0 * faced))).astype(jnp.bfloat16)
-
-    def edge(k, h, side, values):
-        edges[k, h, side] = coupled((elements - 1) * side, aligned(1 - side, 2 * faced), values)
-
-    def inside(k, h, of):
-        for e in range(elements - 1):
-            links[k, h, e, low] = coupled(e + 1, high, of(e + 1))
-            links[k, h, e + 1, high] = coupled(e, low, of(e))
-
-    def given(h):
-        return lambda e: vectors[e, :, h * columns : (h + 1) * columns]
+            edges[k + 1, h, 1 - side] = coupled(e, aligned(side, 2 * faced), state[e, :, held])
+            launch(halo(k + 1, h, 1 - side))
+
+    def edge_pair(k, side, values):
+        e = (elements - 1) * side
+        value = coupled(e, aligned(1 - side, 2 * faced), values)
+        for h in range(2):
+            edges[k, h, side] = value[:, h * columns : (h + 1) * columns]
+            launch(halo(k, h, side))
 
     def far_faces():
         points = points_of(chip)
@@ -554,12 +584,11 @@
         for h in range(2):
             for side in range(2):
                 halo(0, h, side).wait_recv()
-            held = pl.ds(h * columns, columns)
-            for e in range(elements):
-                for q in range(2):
-                    some = slice(q * wide, (q + 1) * wide)
-                    value = applied_by(e, some, q * wide, wide, vectors[e, some, held])
-                    out[e, some, held] = value + through(0, h, e, some, slice(0, 4 * faced))
+        for e in range(elements):
+            for q in range(2):
+                some = slice(q * wide, (q + 1) * wide)
+                value = applied_by(e, some, q * wide, wide, vectors[e, some])
+                out[e, some] = value + through(0, e, some, slice(0, 4 * faced), slice(None))
 
     cross_sum[...] = jnp.zeros(cross_sum.shape, jnp.float32)
     for piece, (k, begin, size) in enumerate(pieces):
@@ -584,12 +613,9 @@
                     cut = faces[e, :, index * faced : (index + 1) * faced]
                     turn = index + 1 - 2 * (index % 2)
                     turned[e, turn * faced : (turn + 1) * faced, :] = cut.T
-            for h in range(2):
-                for side in range(2):
-                    edge(0, h, side, given(h)((elements - 1) * side))
-                    launch(halo(0, h, side))
-            for h in range(2):
-                inside(0, h, given(h))
+            for side in range(2):
+                edge_pair(0, side, vectors[(elements - 1) * side])
+            inside(0, vectors)
             cross_face[...] = diagonal(chip, far)
     final = send(
         cross_sum.at[aligned(1 - core, rows)],
@@ -608,16 +634,13 @@
     def finish(e):
         mine, theirs = aligned(e, wide), aligned(1 - e, wide)
         operator[e, theirs, mine] = operator[e, mine, theirs].T
-        for h in range(2):
-            held = pl.ds(h * columns, columns)
-            for q in range(2):
-                some = slice(q * wide, (q + 1) * wide)
-                rest = slice((1 - q) * wide, (2 - q) * wide)
-                applied = out[e, some, held]
-                applied += applied_by(e, some, (1 - q) * wide, wide, vectors[e, rest, held])
-                update(0, h, e, some, applied)
-            edge(1, h, e, state[h, e])
-            launch(halo(1, h, e))
+        for q in range(2):
+            some = slice(q * wide, (q + 1) * wide)
+            rest = slice((1 - q) * wide, (2 - q) * wide)
+            applied = out[e, some]
+            applied += applied_by(e, some, (1 - q) * wide, wide, vectors[e, rest])
+            update(0, e, some, slice(None), applied)
+        edge_pair(1, e, state[e])
 
     block_copy(0, elements, partner, partner).wait_recv()
     finish(chip)
@@ -625,21 +648,12 @@
         block_copy(d, elements, sources[d], sources[d]).wait_recv()
     finish(far)
 
-    def kept(h):
-        return lambda e: state[h, e]
-
-    for h in range(2):
-        inside(1, h, kept(h))
-        before(1, h)
     for k in range(1, STEPS):
+        inside(k, state)
+        before(k)
         for h in range(2):
             for side in (1 - turn_side, turn_side):
                 after(k, h, side)
-                if k + 1 < STEPS:
-                    launch(halo(k + 1, h, 1 - side))
-            if k + 1 < STEPS:
-                inside(k + 1, h, kept(h))
-                before(k + 1, h)
 
     for copy in sends:
         copy.wait_send()
@@ -677,11 +691,11 @@
             pltpu.VMEM((rows, 2 * rows), f32),
             pltpu.VMEM((elements, rows, 2 * rows), f32),
             pltpu.VMEM((rows, 2 * rows), f32),
-            pltpu.VMEM((2, elements, total, width // 2), bf16),
-            pltpu.VMEM((STEPS, 2, elements, 4 * faced, width // 2), bf16),
+            pltpu.VMEM((elements, total, width), bf16),
+            pltpu.VMEM((STEPS, elements, 4 * faced, width), bf16),
             pltpu.VMEM((STEPS, 2, 2, 2 * faced, width // 2), bf16),
-            pltpu.VMEM((2, elements, total, width // 2), f32),
-            pltpu.VMEM((2, elements, total, width // 2), f32),
+            pltpu.VMEM((elements, total, width), f32),
+            pltpu.VMEM((elements, total, width), f32),
             dma((4,)),
             dma((1 + elements, parts)),
             dma((elements, parts)),
@@ -696,6 +710,7 @@
             dma((inner - 1, elements + 1)),
             dma((STEPS, 2, 2)),
             dma((STEPS, 2, 2)),
+            pltpu.SemaphoreType.REGULAR((2,)),
         ],
         compiler_params=pltpu.CompilerParams(
             collective_id=0, has_side_effects=True, vmem_limit_bytes=60 * 1024 * 1024
@@ -714,7 +729,7 @@
     )
 
     def local(basis, *rest):
-        if inner == 4 and basis.shape[0] == 2:
+        if inner == 4 and basis.shape[0] == 2 and ring >= 4 and ring % 2 == 0:
             return fused(inner, ring, basis, *rest)
         return per_device(basis, *rest)
 

time: 144 us -> 142 us (0.986)
  Pallas kernels: 143 us -> 141 us
    pallas_call x1, Pallas kernels: 143 us -> 141 us  [fused(): pl.pallas_call(functools.partial(assemble_and_filter, inner, ring), out_s...]
where the time goes in v4:
time: 142 us
  Pallas kernels  141 us (99%)
    pallas_call x1, Pallas kernels, fused(): pl.pallas_call(functools.partial(assemble_and_filter, inner, ring), out_s...  141 us

profile of v4, /device:TPU:0, one launch (start us, length us, event | category | flops | bytes accessed | tf_op | source)
XLA Modules:
  0.0 141.7 jit_solution(16209972828851902785)
XLA Ops:
  0.0 140.7 %shard_map.55 = f32[2,512,256]{2,1,0:T(8,128)S(1)} custom-call(bf16[2,4,128,4096]{3,2,1,0:T(8,128)(2,1)} %basis.1, f32[2,4096]{1,0:T(2,128)} %potential_in.1, s32[2,2,128]{2,1,0:T(2,128)} %face_index_in.1, s32[2,128]{1,0:T(2,128)} %face_match_in.1, bf16[2,512,256]{2,1,0:T(8,128)(2,1)} %vectors_in.1), custom_call_target="tpu_custom_call" | custom-call | tf_op jit(solution)/shard_map/pallas_call | solution.py:670
  140.8 1.0 copy.7
